TPU v7x, 32 devices: a whole 2x2x4 slice. The times are simulated.
32 devices in a mesh: sec: 4 (over z), blk: 8 (over y, x, core).
Axes of the slice: x: 2, y: 2, z: 4, core: 2. Of those that a mesh axis runs over, the one named last changes fastest.
Arguments:
- raw: bfloat16 [32, 128, 256], P(('sec', 'blk')), may hold values from -6 to 6
- tissue: int32 [4, 8, 4], P('sec', 'blk'), may hold values 0 or 1
- w_emb: bfloat16 [32, 3, 3], replicated, may hold values from -3 to 3
- w_one: bfloat16 [32, 32, 3, 3], replicated, may hold values from -0.5 to 0.5
- w_down: bfloat16 [64, 32, 2, 2], replicated, may hold values from -0.75 to 0.75
- w_deep: bfloat16 [64, 64, 3, 3, 3], replicated, may hold values from -0.21875 to 0.21875
- w_up: bfloat16 [32, 64, 2, 2], replicated, may hold values from -1 to 1
- w_out: bfloat16 [3, 32], replicated, may hold values from -1 to 1
Outputs:
- logits: float32 [3, 32, 128, 256], P(None, 'sec', 'blk')
Inputs may be any that keep to these rules, and one draw needn't show every extreme that they name: 1 marks a block of 8 sections, 16 columns and one 4-th of the rows that holds tissue, 0 one without.
All inputs are finite; a program needn't handle non-finite values.
Results may differ from a plain program's by a relative error of at most 0.0067.
Values may be sent and summed in bfloat16 or wider, within the bound.
A program may use at most 256 MiB of HBM per device.

v0:
```python
import jax
import jax.numpy as jnp
from jax import lax
from jax.sharding import PartitionSpec as P


def extended(value, sides, width):
    for axis, dim in sides:
        peers, length = (lax.axis_size(axis), value.shape[dim])
        up = [(i, (i + 1) % peers) for i in range(peers - 1)]
        down = [(j, i) for i, j in up]
        last = lax.slice_in_dim(value, length - width, length, axis=dim)
        leading = lax.slice_in_dim(value, 0, width, axis=dim)
        before = lax.ppermute(last, axis, up)
        after = lax.ppermute(leading, axis, down)
        value = jnp.concatenate([before, value, after], axis=dim)
    return value


def embed(padded, w_emb, columns_out, length_y):
    stacked = []
    for offset_x in range(3):
        for offset_y in range(3):
            stacked.append(
                padded[:, offset_x : offset_x + columns_out, offset_y : offset_y + length_y]
            )
    stacked = jnp.stack(stacked, 0)
    weights = w_emb.reshape(w_emb.shape[0], 9)
    summed = jnp.einsum("ck,kzxy->czxy", weights, stacked, preferred_element_type=jnp.float32)
    return jnp.maximum(summed, 0.0).astype(jnp.bfloat16)


def conv_plane(padded, weights, width_x, length_y):
    summed = None
    for offset_x in range(3):
        for offset_y in range(3):
            window = padded[:, :, offset_x : offset_x + width_x, offset_y : offset_y + length_y]
            contribution = jnp.einsum(
                "oc,czxy->ozxy",
                weights[:, :, offset_x, offset_y],
                window,
                preferred_element_type=jnp.float32,
            )
            summed = contribution if summed is None else summed + contribution
    return summed


def conv_volume(padded, weights, depth_z, width_x, length_y):
    summed = None
    for offset_z in range(3):
        for offset_x in range(3):
            for offset_y in range(3):
                window = padded[
                    :,
                    offset_z : offset_z + depth_z,
                    offset_x : offset_x + width_x,
                    offset_y : offset_y + length_y,
                ]
                contribution = jnp.einsum(
                    "oc,czxy->ozxy",
                    weights[:, :, offset_z, offset_x, offset_y],
                    window,
                    preferred_element_type=jnp.float32,
                )
                summed = contribution if summed is None else summed + contribution
    return summed


def per_device(raw, tissue, w_emb, w_one, w_down, w_deep, w_up, w_out):
    sections = lax.all_to_all(raw, "blk", split_axis=1, concat_axis=0, tiled=True)
    depth_z, width_x, length_y = sections.shape
    blocks_y = tissue.shape[2]
    span_y = length_y // blocks_y
    half_x = width_x // 2
    half_y = length_y // 2
    half_span = span_y // 2
    channels = w_emb.shape[0]
    flags = tissue[0, 0].astype(jnp.float32)
    mask_full = jnp.repeat(flags, span_y)
    mask_half = jnp.repeat(flags, half_span)
    masked = sections * mask_full.astype(jnp.bfloat16)
    narrow = extended(masked, (("blk", 1),), 1)
    narrow = jnp.pad(narrow, ((0, 0), (0, 0), (1, 1)))
    local_emb = embed(narrow, w_emb, width_x, length_y)
    embedded = extended(local_emb, (("blk", 2),), 1)
    embedded = jnp.pad(embedded, ((0, 0), (0, 0), (0, 0), (1, 1)))
    first_sum = conv_plane(embedded, w_one, width_x, length_y)
    features = (jnp.maximum(first_sum, 0.0) * mask_full).astype(jnp.bfloat16)
    shaped = features.reshape(channels, depth_z, half_x, 2, half_y, 2)
    lowered = jnp.einsum("ocab,czxayb->ozxy", w_down, shaped, preferred_element_type=jnp.float32)
    down = (jnp.maximum(lowered, 0.0) * mask_half).astype(jnp.bfloat16)
    rimmed = extended(down, (("sec", 1), ("blk", 2)), 1)
    rimmed = jnp.pad(rimmed, ((0, 0), (0, 0), (0, 0), (1, 1)))
    deep_sum = conv_volume(rimmed, w_deep, depth_z, half_x, half_y)
    deep = (jnp.maximum(deep_sum, 0.0) * mask_half).astype(jnp.bfloat16)
    raised = jnp.einsum("ocab,czxy->ozxayb", w_up, deep, preferred_element_type=jnp.float32)
    raised = raised.reshape(channels, depth_z, width_x, length_y)
    decoded = (jnp.maximum(raised + features.astype(jnp.float32), 0.0) * mask_full).astype(
        jnp.bfloat16
    )
    logits = jnp.einsum("oc,czxy->ozxy", w_out, decoded, preferred_element_type=jnp.float32)
    return logits * mask_full


def solution(mesh):
    placed = (P(("sec", "blk"), None, None), P("sec", "blk", None), P(), P(), P(), P(), P(), P())
    return jax.shard_map(
        per_device,
        mesh=mesh,
        in_specs=placed,
        out_specs=P(None, "sec", "blk", None),
        check_vma=False,
    )
```

profile of v0, /device:TPU:11, one launch (start us, length us, event | category | flops | bytes accessed | tf_op | source)
XLA Modules:
  0.0 189.1 jit_solution(16628197516298694183)
XLA Ops:
  3.1 4.6 %all-to-all-start = ((bf16[8,2,2048]{2,1,0:T(2,128)(2,1)}), bf16[8,2,2048]{2,1,0:T(2,128)(2,1)S(1)}, u32[]{:S(2)}, u32[]{:S(2)}) async-start(bf16[8,2,2048]{2,1,0:T(2,128)(2,1)} %reshape.77), calls=%async_computation | async-start | bytes 131072 | tf_op jit(solution)/shard_map/all_to_all | solution.py:70
  11.2 3.5 %collective-permute-start = (bf16[8,1,256]{2,1,0:T(2,128)(2,1)S(1)}, bf16[8,1,256]{2,1,0:T(2,128)(2,1)S(1)}, u32[]{:S(2)}, u32[]{:S(2)}) collective-permute-start(bf16[8,1,256]{2,1,0:T(2,128)(2,1)S(1)} %get-tuple-element.21), channel_id=1, source_target_pairs={{0,1},{1,2},{2,3},{3,4},{4,5},{5,6},{6,7},{8,9},{9,10},{10,11},{11... | collective-permute-start | bytes 12296 | tf_op jit(solution)/shard_map/ppermute | solution.py:14
  14.7 1.9 %collective-permute-start.1 = (bf16[8,1,256]{2,1,0:T(2,128)(2,1)S(1)}, bf16[8,1,256]{2,1,0:T(2,128)(2,1)S(1)}, u32[]{:S(2)}, u32[]{:S(2)}) collective-permute-start(bf16[8,1,256]{2,1,0:T(2,128)(2,1)S(1)} %get-tuple-element.22), channel_id=1, source_target_pairs={{1,0},{2,1},{3,2},{4,3},{5,4},{6,5},{7,6},{9,8},{10,9},{11,10},{12... | collective-permute-start | bytes 12296 | tf_op jit(solution)/shard_map/ppermute | solution.py:15
  16.8 3.8 %collective-permute-done.1 = bf16[8,1,256]{2,1,0:T(2,128)(2,1)S(1)} collective-permute-done((bf16[8,1,256]{2,1,0:T(2,128)(2,1)S(1)}, bf16[8,1,256]{2,1,0:T(2,128)(2,1)S(1)}, u32[]{:S(2)}, u32[]{:S(2)}) %collective-permute-start.1) | collective-permute-done | bytes 4128 | tf_op jit(solution)/shard_map/ppermute | solution.py:15
  21.9 1.8 stack.36
  24.5 1.9 %collective-permute-start.2 = (bf16[32,8,1,256]{3,0,2,1:T(8,128)(2,1)S(1)}, bf16[32,8,1,256]{3,0,2,1:T(8,128)(2,1)S(1)}, u32[]{:S(2)}, u32[]{:S(2)}) collective-permute-start(bf16[32,8,1,256]{3,0,2,1:T(8,128)(2,1)S(1)} %get-tuple-element.5), channel_id=1, source_target_pairs={{0,1},{1,2},{2,3},{3,4},{4,5},{5,6},{6,7},{8,9},{9,10},{10,11},{11... | collective-permute-start | bytes 393224 | tf_op jit(solution)/shard_map/ppermute | solution.py:14
  26.5 2.6 %collective-permute-start.3 = (bf16[32,8,1,256]{3,0,2,1:T(8,128)(2,1)S(1)}, bf16[32,8,1,256]{3,0,2,1:T(8,128)(2,1)S(1)}, u32[]{:S(2)}, u32[]{:S(2)}) collective-permute-start(bf16[32,8,1,256]{3,0,2,1:T(8,128)(2,1)S(1)} %get-tuple-element.6), channel_id=1, source_target_pairs={{1,0},{2,1},{3,2},{4,3},{5,4},{6,5},{7,6},{9,8},{10,9},{11,10},{12... | collective-permute-start | bytes 393224 | tf_op jit(solution)/shard_map/ppermute | solution.py:15
  29.1 2.6 %fusion.175 = f32[8,16,256,32]{2,3,1,0:T(8,128)} fusion(bf16[32,8,16,256]{3,0,2,1:T(8,128)(2,1)S(1)} %fusion.41, bf16[32,32,3,3]{1,0,3,2:T(8,128)(2,1)S(1)} %copy-done.4), kind=kOutput, calls=%fused_computation.206 | convolution fusion | flops 67108864 | bytes 6299648 | tf_op jit(solution)/shard_map/oc,czxy->ozxy/dot_general | solution.py:38
  31.7 2.0 %collective-permute-done.3 = bf16[32,8,1,256]{3,0,2,1:T(8,128)(2,1)S(1)} collective-permute-done((bf16[32,8,1,256]{3,0,2,1:T(8,128)(2,1)S(1)}, bf16[32,8,1,256]{3,0,2,1:T(8,128)(2,1)S(1)}, u32[]{:S(2)}, u32[]{:S(2)}) %collective-permute-start.3) | collective-permute-done | bytes 131104 | tf_op jit(solution)/shard_map/ppermute | solution.py:15
  33.7 2.4 %fusion.8 = bf16[32,8,18,258]{3,0,2,1:T(8,128)(2,1)S(1)} fusion(bf16[32,8,1,256]{3,0,2,1:T(8,128)(2,1)S(1)} %collective-permute-done.3, bf16[32,8,16,256]{3,0,2,1:T(8,128)(2,1)S(1)} %fusion.41, bf16[32,8,1,256]{3,0,2,1:T(8,128)(2,1)S(1)} %collective-permute-done.2), kind=kLoop, calls=%fused_computation.15 | loop fusion | flops 14266368 | bytes 4737024 | tf_op jit(solution)/shard_map/concatenate | solution.py:16
  36.1 2.7 %fusion.20 = f32[8,16,256,32]{2,3,1,0:T(8,128)} fusion(bf16[32,8,18,258]{3,0,2,1:T(8,128)(2,1)S(1)} %fusion.8, bf16[32,32,3,3]{1,0,3,2:T(8,128)(2,1)S(1)} %copy-done.4), kind=kOutput, calls=%fused_computation.29 | convolution fusion | flops 67108864 | bytes 6299648 | tf_op jit(solution)/shard_map/oc,czxy->ozxy/dot_general | solution.py:38
  38.7 2.8 %fusion.22 = f32[8,16,256,32]{2,3,1,0:T(8,128)} fusion(bf16[32,8,18,258]{3,0,2,1:T(8,128)(2,1)S(1)} %fusion.8, bf16[32,32,3,3]{1,0,3,2:T(8,128)(2,1)S(1)} %copy-done.4), kind=kOutput, calls=%fused_computation.31 | convolution fusion | flops 67108864 | bytes 6299648 | tf_op jit(solution)/shard_map/oc,czxy->ozxy/dot_general | solution.py:38
  41.5 2.6 %fusion.24 = f32[8,16,256,32]{2,3,1,0:T(8,128)} fusion(bf16[32,8,18,258]{3,0,2,1:T(8,128)(2,1)S(1)} %fusion.8, bf16[32,32,3,3]{1,0,3,2:T(8,128)(2,1)S(1)} %copy-done.4), kind=kOutput, calls=%fused_computation.33 | convolution fusion | flops 67108864 | bytes 6299648 | tf_op jit(solution)/shard_map/oc,czxy->ozxy/dot_general | solution.py:38
  44.1 2.8 %fusion.26 = f32[8,16,256,32]{2,3,1,0:T(8,128)} fusion(bf16[32,8,18,258]{3,0,2,1:T(8,128)(2,1)S(1)} %fusion.8, bf16[32,32,3,3]{1,0,3,2:T(8,128)(2,1)S(1)} %copy-done.4), kind=kOutput, calls=%fused_computation.35 | convolution fusion | flops 67108864 | bytes 6299648 | tf_op jit(solution)/shard_map/oc,czxy->ozxy/dot_general | solution.py:38
  46.9 2.7 %fusion.30 = f32[8,16,256,32]{2,3,1,0:T(8,128)} fusion(bf16[32,8,18,258]{3,0,2,1:T(8,128)(2,1)S(1)} %fusion.8, bf16[32,32,3,3]{1,0,3,2:T(8,128)(2,1)S(1)} %copy-done.4), kind=kOutput, calls=%fused_computation.40 | convolution fusion | flops 67108864 | bytes 6299648 | tf_op jit(solution)/shard_map/oc,czxy->ozxy/dot_general | solution.py:38
  50.3 2.6 %fusion.18 = f32[8,16,256,32]{2,3,1,0:T(8,128)} fusion(bf16[32,8,1,256]{3,0,2,1:T(8,128)(2,1)S(1)} %collective-permute-done.3, bf16[32,8,16,256]{3,0,2,1:T(8,128)(2,1)S(1)} %fusion.41, bf16[32,32,3,3]{1,0,3,2:T(8,128)(2,1)S(1)} %copy-done.4), kind=kOutput, calls=%fused_computation.27 | convolution fusion | flops 71303168 | bytes 6430720 | tf_op jit(solution)/shard_map/oc,czxy->ozxy/dot_general | solution.py:38
  52.9 10.9 %fusion.38 = bf16[32,8,16,256]{3,0,2,1:T(8,128)(2,1)S(1)} fusion(f32[256]{0:T(256)S(1)} %reshape.30, bf16[32,8,18,258]{3,0,2,1:T(8,128)(2,1)S(1)} %fusion.8, f32[8,16,256,32]{2,3,1,0:T(8,128)} %fusion.18, f32[8,16,256,32]{2,3,1,0:T(8,128)} %fusion.20, f32[8,16,256,32]{2,3,1,0:T(8,128)} %fusion.22, f32[8,16,256,32]{2,3,1,0:T(8,128)} %fusion.175, ...), kind=kOutput, calls=%fused_computation.59 | convolution fusion | flops 78643200 | bytes 37757952 | tf_op jit(solution)/shard_map/oc,czxy->ozxy/dot_general | solution.py:38
  63.9 6.7 %copy.169 = bf16[32,8,16,256]{0,1,3,2:T(8,128)(2,1)} copy(bf16[32,8,16,256]{3,0,2,1:T(8,128)(2,1)S(1)} %fusion.38) | data formatting | bytes 4194304 | tf_op jit(solution)/shard_map/convert_element_type | solution.py:88
  70.5 6.3 %fusion.45 = bf16[64,8,8,128]{3,0,2,1:T(8,128)(2,1)S(1)} fusion(bf16[32,8,8,2,128,2]{0,1,5,4,3,2:T(8,128)(2,1)} %bitcast.394, f32[128]{0:T(128)S(1)} %mul.67, bf16[64,32,2,2,1,1]{0,3,2,1,5,4:T(2,128)(2,1)S(1)} %bitcast.399), kind=kOutput, calls=%fused_computation.64 | convolution fusion | flops 135790592 | bytes 3162624 | tf_op jit(solution)/shard_map/ocab,czxayb->ozxy/dot_general | solution.py:90
  76.8 3.2 %collective-permute-start.4 = (bf16[64,1,8,128]{3,0,2,1:T(8,128)(2,1)S(1)}, bf16[64,1,8,128]{3,0,2,1:T(8,128)(2,1)S(1)}, u32[]{:S(2)}, u32[]{:S(2)}) collective-permute-start(bf16[64,1,8,128]{3,0,2,1:T(8,128)(2,1)S(1)} %get-tuple-element.11), channel_id=1, source_target_pairs={{0,8},{8,16},{16,24},{1,9},{9,17},{17,25},{2,10},{10,18},{18,26},{... | collective-permute-start | bytes 393224 | tf_op jit(solution)/shard_map/ppermute | solution.py:14
  80.0 2.1 %collective-permute-start.5 = (bf16[64,1,8,128]{3,0,2,1:T(8,128)(2,1)S(1)}, bf16[64,1,8,128]{3,0,2,1:T(8,128)(2,1)S(1)}, u32[]{:S(2)}, u32[]{:S(2)}) collective-permute-start(bf16[64,1,8,128]{3,0,2,1:T(8,128)(2,1)S(1)} %get-tuple-element.12), channel_id=1, source_target_pairs={{8,0},{16,8},{24,16},{9,1},{17,9},{25,17},{10,2},{18,10},{26,18},{... | collective-permute-start | bytes 393224 | tf_op jit(solution)/shard_map/ppermute | solution.py:15
  83.9 2.1 %collective-permute-done.5 = bf16[64,1,8,128]{3,0,2,1:T(8,128)(2,1)S(1)} collective-permute-done((bf16[64,1,8,128]{3,0,2,1:T(8,128)(2,1)S(1)}, bf16[64,1,8,128]{3,0,2,1:T(8,128)(2,1)S(1)}, u32[]{:S(2)}, u32[]{:S(2)}) %collective-permute-start.5) | collective-permute-done | bytes 131104 | tf_op jit(solution)/shard_map/ppermute | solution.py:15
  86.0 3.4 %collective-permute-start.6 = (bf16[64,10,1,128]{3,0,2,1:T(8,128)(2,1)S(1)}, bf16[64,10,1,128]{3,0,2,1:T(8,128)(2,1)S(1)}, u32[]{:S(2)}, u32[]{:S(2)}) collective-permute-start(bf16[64,10,1,128]{3,0,2,1:T(8,128)(2,1)S(1)} %get-tuple-element.9), channel_id=1, source_target_pairs={{0,1},{1,2},{2,3},{3,4},{4,5},{5,6},{6,7},{8,9},{9,10},{10,11},{11... | collective-permute-start | bytes 491528 | tf_op jit(solution)/shard_map/ppermute | solution.py:14
  89.4 1.9 %collective-permute-start.7 = (bf16[64,10,1,128]{3,0,2,1:T(8,128)(2,1)S(1)}, bf16[64,10,1,128]{3,0,2,1:T(8,128)(2,1)S(1)}, u32[]{:S(2)}, u32[]{:S(2)}) collective-permute-start(bf16[64,10,1,128]{3,0,2,1:T(8,128)(2,1)S(1)} %get-tuple-element.10), channel_id=1, source_target_pairs={{1,0},{2,1},{3,2},{4,3},{5,4},{6,5},{7,6},{9,8},{10,9},{11,10},{12... | collective-permute-start | bytes 491528 | tf_op jit(solution)/shard_map/ppermute | solution.py:15
  91.3 1.8 fusion.58
  94.8 2.1 %collective-permute-done.7 = bf16[64,10,1,128]{3,0,2,1:T(8,128)(2,1)S(1)} collective-permute-done((bf16[64,10,1,128]{3,0,2,1:T(8,128)(2,1)S(1)}, bf16[64,10,1,128]{3,0,2,1:T(8,128)(2,1)S(1)}, u32[]{:S(2)}, u32[]{:S(2)}) %collective-permute-start.7) | collective-permute-done | bytes 163872 | tf_op jit(solution)/shard_map/ppermute | solution.py:15
  96.9 3.1 %select_maximum_fusion = bf16[64,10,10,130]{3,0,2,1:T(8,128)(2,1)S(1)} fusion(bf16[64,10,1,128]{3,0,2,1:T(8,128)(2,1)S(1)} %collective-permute-done.7, bf16[64,10,1,128]{3,0,2,1:T(8,128)(2,1)S(1)} %collective-permute-done.6, bf16[64,1,8,128]{3,0,2,1:T(8,128)(2,1)S(1)} %collective-permute-done.5, bf16[64,8,8,128]{3,0,2,1:T(8,128)(2,1)S(1)} %fusion.45, ...), kind=kLoop, calls=%fused_computation.16 | loop fusion | flops 14976000 | bytes 3302400 | tf_op jit(solution)/shard_map/concatenate | solution.py:16
  101.7 1.9 %fusion.56 = f32[8,8,128,64]{2,3,1,0:T(8,128)} fusion(bf16[64,10,10,130]{3,0,2,1:T(8,128)(2,1)S(1)} %select_maximum_fusion, bf16[64,64,3,3,3]{1,0,4,3,2:T(8,128)(2,1)S(1)} %copy-done.3), kind=kOutput, calls=%fused_computation.72 | convolution fusion | flops 67108864 | bytes 3162112 | tf_op jit(solution)/shard_map/oc,czxy->ozxy/dot_general | solution.py:59
  103.6 1.8 fusion.60
  105.4 1.9 fusion.62
  109.0 1.9 %fusion.68 = f32[8,8,128,64]{2,3,1,0:T(8,128)} fusion(bf16[64,10,10,130]{3,0,2,1:T(8,128)(2,1)S(1)} %select_maximum_fusion, bf16[64,64,3,3,3]{1,0,4,3,2:T(8,128)(2,1)S(1)} %copy-done.3), kind=kOutput, calls=%fused_computation.85 | convolution fusion | flops 67108864 | bytes 3162112 | tf_op jit(solution)/shard_map/oc,czxy->ozxy/dot_general | solution.py:59
  110.9 1.7 fusion.72
  112.7 1.9 fusion.74
  116.3 1.9 %fusion.78 = f32[8,8,128,64]{2,3,1,0:T(8,128)} fusion(bf16[64,10,10,130]{3,0,2,1:T(8,128)(2,1)S(1)} %select_maximum_fusion, bf16[64,64,3,3,3]{1,0,4,3,2:T(8,128)(2,1)S(1)} %copy-done.3), kind=kOutput, calls=%fused_computation.95 | convolution fusion | flops 67108864 | bytes 3162112 | tf_op jit(solution)/shard_map/oc,czxy->ozxy/dot_general | solution.py:59
  118.2 1.8 fusion.82
  120.0 1.9 %fusion.84 = f32[8,8,128,64]{2,3,1,0:T(8,128)} fusion(bf16[64,10,10,130]{3,0,2,1:T(8,128)(2,1)S(1)} %select_maximum_fusion, bf16[64,64,3,3,3]{1,0,4,3,2:T(8,128)(2,1)S(1)} %copy-done.3), kind=kOutput, calls=%fused_computation.101 | convolution fusion | flops 67108864 | bytes 3162112 | tf_op jit(solution)/shard_map/oc,czxy->ozxy/dot_general | solution.py:59
  121.9 1.8 fusion.88
  123.6 1.9 fusion.90
  125.5 1.8 fusion.94
  127.3 1.8 fusion.96
  129.1 1.8 fusion.100
  131.4 1.8 fusion.64
  134.9 1.8 fusion.98
  138.4 1.8 fusion.70
  141.9 20.8 %convolution_bitcast_fusion = f32[32,8,8,2,128,2]{4,0,5,3,2,1:T(8,128)} fusion(f32[8,8,128,64]{2,3,1,0:T(8,128)} %fusion.52, f32[8,8,128,64]{2,3,1,0:T(8,128)} %fusion.54, f32[8,8,128,64]{2,3,1,0:T(8,128)} %fusion.56, f32[8,8,128,64]{2,3,1,0:T(8,128)} %fusion.58, f32[8,8,128,64]{2,3,1,0:T(8,128)} %fusion.60, f32[8,8,128,64]{2,3,1,0:T(8,128)} %fusion.62, ...), kind=kOutput, calls=%fused_computation.23 | convolution fusion | flops 216530944 | bytes 59818496 | tf_op jit(solution)/shard_map/ocab,czxy->ozxayb/dot_general | solution.py:96
  162.8 11.0 %copy.173 = f32[32,8,8,2,128,2]{0,1,5,4,3,2:T(8,128)} copy(f32[32,8,8,2,128,2]{4,0,5,3,2,1:T(8,128)} %convolution_bitcast_fusion) | data formatting | bytes 8388608 | tf_op jit(solution)/shard_map/ocab,czxy->ozxayb/transpose | solution.py:96
  173.7 11.5 %copy.174 = f32[32,8,16,256]{3,0,2,1:T(8,128)} copy(f32[32,8,16,256]{0,1,3,2:T(8,128)} %bitcast.393) | data formatting | bytes 8388608 | tf_op jit(solution)/shard_map/reshape | solution.py:97
  185.3 2.9 %fusion.49 = f32[3,8,16,256]{3,0,2,1:T(4,128)S(1)} fusion(f32[32,8,16,256]{3,0,2,1:T(8,128)} %copy.174, bf16[32,8,16,256]{3,0,2,1:T(8,128)(2,1)S(1)} %copy-done.2, f32[256]{0:T(256)S(1)} %reshape.30, bf16[3,32]{1,0:T(4,128)(2,1)S(1)} %copy-done.5), kind=kOutput, calls=%fused_computation.66 | convolution fusion | flops 11632640 | bytes 6685888 | tf_op jit(solution)/shard_map/oc,czxy->ozxy/dot_general | solution.py:101
  (61 shorter events, 24.5 us)
Async XLA Ops:
  0.0 141.9 %copy-start = (bf16[32,64,2,2]{1,3,2,0:T(2,128)(2,1)S(1)}, bf16[32,64,2,2]{1,3,2,0:T(2,128)(2,1)}, u32[]{:S(2)}) copy-start(bf16[32,64,2,2]{1,3,2,0:T(2,128)(2,1)} %param.14) | copy-start | bytes 49156
  3.1 7.9 %all-to-all-start = ((bf16[8,2,2048]{2,1,0:T(2,128)(2,1)}), bf16[8,2,2048]{2,1,0:T(2,128)(2,1)S(1)}, u32[]{:S(2)}, u32[]{:S(2)}) async-start(bf16[8,2,2048]{2,1,0:T(2,128)(2,1)} %reshape.77), calls=%async_computation | async-start | bytes 131072 | tf_op jit(solution)/shard_map/all_to_all | solution.py:70
  11.2 5.6 %collective-permute-start = (bf16[8,1,256]{2,1,0:T(2,128)(2,1)S(1)}, bf16[8,1,256]{2,1,0:T(2,128)(2,1)S(1)}, u32[]{:S(2)}, u32[]{:S(2)}) collective-permute-start(bf16[8,1,256]{2,1,0:T(2,128)(2,1)S(1)} %get-tuple-element.21), channel_id=1, source_target_pairs={{0,1},{1,2},{2,3},{3,4},{4,5},{5,6},{6,7},{8,9},{9,10},{10,11},{11... | collective-permute-start | bytes 12296 | tf_op jit(solution)/shard_map/ppermute | solution.py:14
  14.7 5.9 %collective-permute-start.1 = (bf16[8,1,256]{2,1,0:T(2,128)(2,1)S(1)}, bf16[8,1,256]{2,1,0:T(2,128)(2,1)S(1)}, u32[]{:S(2)}, u32[]{:S(2)}) collective-permute-start(bf16[8,1,256]{2,1,0:T(2,128)(2,1)S(1)} %get-tuple-element.22), channel_id=1, source_target_pairs={{1,0},{2,1},{3,2},{4,3},{5,4},{6,5},{7,6},{9,8},{10,9},{11,10},{12... | collective-permute-start | bytes 12296 | tf_op jit(solution)/shard_map/ppermute | solution.py:15
  23.7 5.3 %copy-start.4 = (bf16[32,32,3,3]{1,0,3,2:T(8,128)(2,1)S(1)}, bf16[32,32,3,3]{1,0,3,2:T(8,128)(2,1)}, u32[]{:S(2)}) copy-start(bf16[32,32,3,3]{1,0,3,2:T(8,128)(2,1)} %param.11) | copy-start | bytes 55300
  24.5 7.2 %collective-permute-start.2 = (bf16[32,8,1,256]{3,0,2,1:T(8,128)(2,1)S(1)}, bf16[32,8,1,256]{3,0,2,1:T(8,128)(2,1)S(1)}, u32[]{:S(2)}, u32[]{:S(2)}) collective-permute-start(bf16[32,8,1,256]{3,0,2,1:T(8,128)(2,1)S(1)} %get-tuple-element.5), channel_id=1, source_target_pairs={{0,1},{1,2},{2,3},{3,4},{4,5},{5,6},{6,7},{8,9},{9,10},{10,11},{11... | collective-permute-start | bytes 393224 | tf_op jit(solution)/shard_map/ppermute | solution.py:14
  26.5 7.2 %collective-permute-start.3 = (bf16[32,8,1,256]{3,0,2,1:T(8,128)(2,1)S(1)}, bf16[32,8,1,256]{3,0,2,1:T(8,128)(2,1)S(1)}, u32[]{:S(2)}, u32[]{:S(2)}) collective-permute-start(bf16[32,8,1,256]{3,0,2,1:T(8,128)(2,1)S(1)} %get-tuple-element.6), channel_id=1, source_target_pairs={{1,0},{2,1},{3,2},{4,3},{5,4},{6,5},{7,6},{9,8},{10,9},{11,10},{12... | collective-permute-start | bytes 393224 | tf_op jit(solution)/shard_map/ppermute | solution.py:15
  63.8 6.7 %copy-start.1 = (bf16[32,8,16,256]{3,0,2,1:T(8,128)(2,1)}, bf16[32,8,16,256]{3,0,2,1:T(8,128)(2,1)S(1)}, u32[]{:S(2)}) copy-start(bf16[32,8,16,256]{3,0,2,1:T(8,128)(2,1)S(1)} %fusion.38) | copy-start | bytes 6291460
  63.8 6.7 %copy-start.6 = (bf16[64,32,2,2]{0,3,2,1:T(2,128)(2,1)S(1)}, bf16[64,32,2,2]{0,3,2,1:T(2,128)(2,1)}, u32[]{:S(2)}) copy-start(bf16[64,32,2,2]{0,3,2,1:T(2,128)(2,1)} %param.12) | copy-start | bytes 49156
  70.5 11.6 %copy-start.3 = (bf16[64,64,3,3,3]{1,0,4,3,2:T(8,128)(2,1)S(1)}, bf16[64,64,3,3,3]{1,0,4,3,2:T(8,128)(2,1)}, u32[]{:S(2)}) copy-start(bf16[64,64,3,3,3]{1,0,4,3,2:T(8,128)(2,1)} %param.13) | copy-start | bytes 663556
  76.8 7.0 %collective-permute-start.4 = (bf16[64,1,8,128]{3,0,2,1:T(8,128)(2,1)S(1)}, bf16[64,1,8,128]{3,0,2,1:T(8,128)(2,1)S(1)}, u32[]{:S(2)}, u32[]{:S(2)}) collective-permute-start(bf16[64,1,8,128]{3,0,2,1:T(8,128)(2,1)S(1)} %get-tuple-element.11), channel_id=1, source_target_pairs={{0,8},{8,16},{16,24},{1,9},{9,17},{17,25},{2,10},{10,18},{18,26},{... | collective-permute-start | bytes 393224 | tf_op jit(solution)/shard_map/ppermute | solution.py:14
  80.0 5.9 %collective-permute-start.5 = (bf16[64,1,8,128]{3,0,2,1:T(8,128)(2,1)S(1)}, bf16[64,1,8,128]{3,0,2,1:T(8,128)(2,1)S(1)}, u32[]{:S(2)}, u32[]{:S(2)}) collective-permute-start(bf16[64,1,8,128]{3,0,2,1:T(8,128)(2,1)S(1)} %get-tuple-element.12), channel_id=1, source_target_pairs={{8,0},{16,8},{24,16},{9,1},{17,9},{25,17},{10,2},{18,10},{26,18},{... | collective-permute-start | bytes 393224 | tf_op jit(solution)/shard_map/ppermute | solution.py:15
  86.0 8.8 %collective-permute-start.6 = (bf16[64,10,1,128]{3,0,2,1:T(8,128)(2,1)S(1)}, bf16[64,10,1,128]{3,0,2,1:T(8,128)(2,1)S(1)}, u32[]{:S(2)}, u32[]{:S(2)}) collective-permute-start(bf16[64,10,1,128]{3,0,2,1:T(8,128)(2,1)S(1)} %get-tuple-element.9), channel_id=1, source_target_pairs={{0,1},{1,2},{2,3},{3,4},{4,5},{5,6},{6,7},{8,9},{9,10},{10,11},{11... | collective-permute-start | bytes 491528 | tf_op jit(solution)/shard_map/ppermute | solution.py:14
  89.4 7.5 %collective-permute-start.7 = (bf16[64,10,1,128]{3,0,2,1:T(8,128)(2,1)S(1)}, bf16[64,10,1,128]{3,0,2,1:T(8,128)(2,1)S(1)}, u32[]{:S(2)}, u32[]{:S(2)}) collective-permute-start(bf16[64,10,1,128]{3,0,2,1:T(8,128)(2,1)S(1)} %get-tuple-element.10), channel_id=1, source_target_pairs={{1,0},{2,1},{3,2},{4,3},{5,4},{6,5},{7,6},{9,8},{10,9},{11,10},{12... | collective-permute-start | bytes 491528 | tf_op jit(solution)/shard_map/ppermute | solution.py:15
  173.7 11.5 %copy-start.2 = (bf16[32,8,16,256]{3,0,2,1:T(8,128)(2,1)S(1)}, bf16[32,8,16,256]{3,0,2,1:T(8,128)(2,1)}, u32[]{:S(2)}) copy-start(bf16[32,8,16,256]{3,0,2,1:T(8,128)(2,1)} %copy-done.1) | copy-start | bytes 6291460
  173.7 11.5 %copy-start.5 = (bf16[3,32]{1,0:T(4,128)(2,1)S(1)}, bf16[3,32]{1,0:T(4,128)(2,1)}, u32[]{:S(2)}) copy-start(bf16[3,32]{1,0:T(4,128)(2,1)} %param.15) | copy-start | bytes 580
where the time goes:
time: 190 us; the launch traced here: 189 us
  matrix products  108 us (57%)
  local copies, waits for them, and re-layouts  36.2 us (19%)
  starting transfers between devices  25.1 us (13%)
  waiting for transfers between devices  11.6 us (6%)
  other arithmetic  7.97 us (4%)
    dot_general x26, matrix products, conv_volume(): jnp.einsum('oc,czxy->ozxy', weights[:, :, offset_z, offset_x, offset_y],...  46.6 us
    dot_general x9, matrix products, conv_plane(): jnp.einsum('oc,czxy->ozxy', weights[:, :, offset_x, offset_y], window, pr...  30.4 us
    dot_general x1, matrix products, per_device(): jnp.einsum('ocab,czxy->ozxayb', w_up, deep, preferred_element_type=jnp.fl...  20.8 us
    ppermute x4, starting transfers between devices, extended(): before = lax.ppermute(last, axis, up)  12.1 us
    reshape x1, local copies, waits for them, and re-layouts, per_device(): raised = raised.reshape(channels, depth_z, width_x, length_y)  11.5 us
    transpose x1, local copies, waits for them, and re-layouts, per_device(): jnp.einsum('ocab,czxy->ozxayb', w_up, deep, preferred_element_type=jnp.fl...  11 us
    ppermute x4, waiting for transfers between devices, extended(): after = lax.ppermute(leading, axis, down)  9.95 us
    ppermute x4, starting transfers between devices, extended(): after = lax.ppermute(leading, axis, down)  8.49 us
  transfers between devices with their start and end apart: 9, of which 5 were waited for; matrix products, arithmetic and copies ran while one was open for 5% of the time, Pallas kernels for 0%

commit v1 on v0

v1 whole, which is shorter than its diff:
```python
import functools

import jax
import jax.numpy as jnp
from jax import lax
from jax.experimental import pallas as pl
from jax.experimental.pallas import tpu as pltpu
from jax.sharding import PartitionSpec as P

F32 = jnp.float32
BF16 = jnp.bfloat16
MESH = pl.DeviceIdType.MESH
NT = (((1,), (1,)), ((), ()))


def exchange_kernel(
    ns, nb, raw_ref, tissue_ref, recv_ref, masks_ref, stage, mine, send_sem, recv_sem, up_sem,
    mask_send, mask_recv, local_sem
):
    sec = lax.axis_index("sec")
    blk = lax.axis_index("blk")
    has_below = sec > 0
    has_above = sec < ns - 1

    barrier = pltpu.get_barrier_semaphore()
    for k in range(1, nb):
        pl.semaphore_signal(
            barrier, inc=1, device_id=(sec, lax.rem(blk + k, nb)), device_id_type=MESH
        )

    @pl.when(has_below)
    def _():
        for k in range(nb):
            pl.semaphore_signal(barrier, inc=1, device_id=(sec - 1, k), device_id_type=MESH)

    @pl.when(has_above)
    def _():
        for k in range(nb):
            pl.semaphore_signal(barrier, inc=1, device_id=(sec + 1, k), device_id_type=MESH)

    section = raw_ref[0].astype(F32)
    nothing = jnp.zeros((8, section.shape[1]), F32)
    for k in range(nb):
        low, high = max(16 * k - 4, 0), min(16 * k + 20, 16 * nb)
        parts = [section[low:high], nothing]
        if k == 0:
            parts = [nothing[:4]] + parts
        if k == nb - 1:
            parts = parts + [nothing[:4]]
        stage[k] = jnp.concatenate(parts, axis=0).astype(BF16)
    for row in range(4):
        value = tissue_ref[0, 0, row].astype(F32)
        mine[row : row + 1, :] = jnp.full((1, 128), value, F32)
    mine[4:8, :] = jnp.zeros((4, 128), F32)
    masks_ref[4] = mine[...]

    @pl.when(jnp.logical_not(has_below))
    def _():
        recv_ref[0] = jnp.zeros(recv_ref.shape[1:], BF16)

    @pl.when(jnp.logical_not(has_above))
    def _():
        recv_ref[nb + 1] = jnp.zeros(recv_ref.shape[1:], BF16)

    local = pltpu.make_async_copy(stage.at[blk], recv_ref.at[blk + 1], local_sem)
    local.start()

    count = (nb - 1) + nb * has_below.astype(jnp.int32) + nb * has_above.astype(jnp.int32)
    pl.semaphore_wait(barrier, count)

    send_up = jnp.logical_and(has_above, blk == nb - 1)
    send_down = jnp.logical_and(has_below, blk == 0)

    def outer(target, slot, sem, k):
        return pltpu.make_async_remote_copy(
            src_ref=stage.at[k],
            dst_ref=recv_ref.at[slot],
            send_sem=up_sem.at[k],
            recv_sem=recv_sem.at[sem],
            device_id=(target, k),
            device_id_type=MESH,
        )

    @pl.when(send_up)
    def _():
        for k in range(nb):
            outer(sec + 1, 0, nb, k).start()

    @pl.when(send_down)
    def _():
        for k in range(nb):
            outer(sec - 1, nb + 1, nb + 1, k).start()

    copies = []
    for k in range(1, nb):
        target = lax.rem(blk + k, nb)
        copy = pltpu.make_async_remote_copy(
            src_ref=stage.at[target],
            dst_ref=recv_ref.at[blk + 1],
            send_sem=send_sem.at[k],
            recv_sem=recv_sem.at[k],
            device_id=(sec, target),
            device_id_type=MESH,
        )
        copy.start()
        copies.append(copy)

    def present(es, eb):
        ok = None
        for at, step, count_of in ((sec, es, ns), (blk, eb, nb)):
            if step == 0:
                continue
            term = at > 0 if step < 0 else at < count_of - 1
            ok = term if ok is None else jnp.logical_and(ok, term)
        return ok

    def mask_copy(es, eb):
        slot = (1 - es) * 3 + (1 - eb)
        return pltpu.make_async_remote_copy(
            src_ref=mine,
            dst_ref=masks_ref.at[slot],
            send_sem=mask_send.at[slot],
            recv_sem=mask_recv.at[slot],
            device_id=(sec + es, blk + eb),
            device_id_type=MESH,
        )

    around = [(es, eb) for es in (-1, 0, 1) for eb in (-1, 0, 1) if (es, eb) != (0, 0)]
    for es, eb in around:

        @pl.when(present(es, eb))
        def _(es=es, eb=eb):
            mask_copy(es, eb).start()

        @pl.when(jnp.logical_not(present(es, eb)))
        def _(es=es, eb=eb):
            masks_ref[(1 + es) * 3 + (1 + eb)] = jnp.zeros((8, 128), F32)

    for es, eb in around:

        @pl.when(present(es, eb))
        def _(es=es, eb=eb):
            mask_copy(es, eb).wait_send()
            mask_copy(-es, -eb).wait_recv()

    local.wait()
    for copy in copies:
        copy.wait_send()
        copy.wait_recv()

    @pl.when(send_up)
    def _():
        for k in range(nb):
            outer(sec + 1, 0, nb, k).wait_send()

    @pl.when(send_down)
    def _():
        for k in range(nb):
            outer(sec - 1, nb + 1, nb + 1, k).wait_send()

    @pl.when(has_below)
    def _():
        outer(sec - 1, 0, nb, 0).wait_recv()

    @pl.when(has_above)
    def _():
        outer(sec + 1, nb + 1, nb + 1, 0).wait_recv()


def exchange(raw, tissue, ns, nb):
    length_y = raw.shape[2]
    return pl.pallas_call(
        functools.partial(exchange_kernel, ns, nb),
        out_shape=(
            jax.ShapeDtypeStruct((nb + 2, 32, length_y), BF16),
            jax.ShapeDtypeStruct((9, 8, 128), F32),
        ),
        in_specs=[
            pl.BlockSpec(memory_space=pltpu.VMEM),
            pl.BlockSpec(memory_space=pltpu.SMEM),
        ],
        out_specs=(pl.BlockSpec(memory_space=pltpu.VMEM), pl.BlockSpec(memory_space=pltpu.VMEM)),
        scratch_shapes=[
            pltpu.VMEM((nb, 32, length_y), BF16),
            pltpu.VMEM((8, 128), F32),
            pltpu.SemaphoreType.DMA((nb,)),
            pltpu.SemaphoreType.DMA((nb + 2,)),
            pltpu.SemaphoreType.DMA((nb,)),
            pltpu.SemaphoreType.DMA((9,)),
            pltpu.SemaphoreType.DMA((9,)),
            pltpu.SemaphoreType.DMA,
        ],
        compiler_params=pltpu.CompilerParams(collective_id=0, has_side_effects=True),
        name="exchange",
    )(raw, tissue)


def iota(shape, dim):
    return lax.broadcasted_iota(jnp.int32, shape, dim)


def dot(a, b):
    return jnp.dot(a, b, preferred_element_type=F32)


def network_kernel(
    nb, recv_ref, masks_ref, emb_ref, one_ref, down_ref, deep_ref, up_ref, out_w_ref, blk_ref,
    logits_ref, perm4, perm_out, w_e, w_c, w_h, w_d0, w_d1, w_d2, w_z, w_u, w_o, deep_t, one_t,
    planes, feats, tall, downs, decoded
):
    nz = nb
    lane = iota((1, 128), 1)

    def put(dst, row, rows, tile, size, blocks):
        total = None
        for q, block in enumerate(blocks):
            if block is None:
                continue
            if total is None:
                total = jnp.where(lane // size == q, block(), 0.0)
            else:
                total = jnp.where(lane // size == q, block(), total)
        if total is None:
            total = jnp.zeros((rows, 128), F32)
        dst[row : row + rows, 128 * tile : 128 * tile + 128] = total.astype(BF16)

    y_of = iota((512, 256), 0)
    perm4[...] = jnp.where(
        iota((512, 256), 1) == 2 * (y_of % 128) - 1 + y_of // 128, 1.0, 0.0
    ).astype(BF16)
    row_of = iota((256, 256), 0)
    perm_out[...] = jnp.where(
        iota((256, 256), 1) == 2 * (row_of % 128) + row_of // 128, 1.0, 0.0
    ).astype(BF16)

    first_x = 16 * blk_ref[0]
    for tile in range(6):
        x_of = lane // 32 + (4 * tile - 1 if tile < 5 else -3)
        inside = jnp.logical_and(x_of + first_x >= 0, x_of + first_x < 16 * nb)
        for b in range(3):
            total = jnp.zeros((32, 128), F32)
            for a in range(3):
                weight = emb_ref[a * 3 + b : a * 3 + b + 1, :].astype(F32)
                hit = jnp.logical_and(iota((32, 128), 0) == x_of + a + 3, inside)
                total = jnp.where(hit, weight, total)
            w_e[32 * b : 32 * b + 32, 128 * tile : 128 * tile + 128] = total.astype(BF16)
    w_e[96:128, :] = jnp.zeros((32, 768), BF16)

    eye = jnp.where(iota((64, 64), 0) == iota((64, 64), 1), 1.0, 0.0).astype(BF16)
    eye32 = jnp.where(iota((32, 32), 0) == iota((32, 32), 1), 1.0, 0.0).astype(BF16)
    for s in range(3):
        for a in range(3):
            for b in range(3):
                block = deep_ref[s, a, b]
                deep_t[(s * 3 + b) * 3 + a] = lax.dot_general(
                    eye, jnp.concatenate([block, block], axis=0), NT, preferred_element_type=F32
                )
    for a in range(3):
        for b in range(3):
            block = one_ref[a, b]
            one_t[b * 3 + a] = lax.dot_general(
                eye32, jnp.concatenate([block] * 4, axis=0), NT, preferred_element_type=F32
            )

    def one_block(b, a):
        return (lambda: one_t[b * 3 + a]) if 0 <= a <= 2 else None

    for b in range(3):
        for e in range(12):
            for tile in range(2):
                blocks = [one_block(b, e - 4 * tile - q) for q in range(4)]
                put(w_c, (b * 12 + e) * 32, 32, tile, 32, blocks)
        for e in range(4):
            pair = [one_block(b, e), one_block(b, e - 1)]
            put(w_h, (b * 8 + e) * 32, 32, 0, 32, [None, None] + pair)
            put(w_h, (b * 8 + 4 + e) * 32, 32, 0, 32, pair + [None, None])

    def down_block(p, x, half):
        a = x - 2 * half
        return (lambda: down_ref[p * 2 + a].astype(F32)) if 0 <= a <= 1 else None

    rims = [-2, -1, 16, 17]
    for dst, columns, halves in (
        (w_d0, list(range(8)) + rims, [-1, 0, 1, 2]),
        (w_d1, list(range(4, 16)), [3, 4, 5, 6]),
        (w_d2, list(range(12, 16)) + rims, [7, 8]),
    ):
        for p in range(2):
            for at, x in enumerate(columns):
                for tile in range(len(halves) // 2):
                    blocks = [down_block(p, x, halves[2 * tile + q]) for q in range(2)]
                    put(dst, (p * len(columns) + at) * 32, 32, tile, 64, blocks)

    def deep_block(s, b, a):
        return (lambda: deep_t[(s * 3 + b) * 3 + a]) if 0 <= a <= 2 else None

    for s in range(3):
        for b in range(3):
            for e in range(6):
                for tile in range(2):
                    blocks = [deep_block(s, b, e - 2 * tile - q) for q in range(2)]
                    put(w_z, ((s * 3 + b) * 6 + e) * 64, 64, tile, 64, blocks)

    for p in range(2):
        block = up_ref[p]
        turned = lax.dot_general(
            eye, jnp.concatenate([block, block], axis=0), NT, preferred_element_type=F32
        )
        for i in range(4):
            for tile in range(2):
                blocks = [(lambda: turned) if i == 2 * tile + q else None for q in range(2)]
                put(w_u, i * 64, 64, p * 2 + tile, 64, blocks)

    for tile in range(4):
        for d in range(3):
            weight = out_w_ref[d : d + 1, :].astype(F32)
            w_o[16 * d : 16 * d + 16, 128 * tile : 128 * tile + 128] = jnp.where(
                iota((16, 128), 0) == lane // 32 + 4 * tile, weight, 0.0
            ).astype(BF16)

    for u in range(2):
        tall[u, 0:8, :] = jnp.zeros((8, 640), F32)
        tall[u, 136:144, :] = jnp.zeros((8, 640), F32)

    @pl.loop(0, (nz + 2) // 2)
    def _(step):
        marks = []
        shifted = []
        for u in range(2):
            z = 2 * step + u
            zone = jnp.where(z == 0, 0, jnp.where(z == nz + 1, 2, 1))
            three = [masks_ref[zone * 3 + k] for k in range(3)]
            marks.append(three)

            def along(m):
                return jnp.concatenate(
                    [
                        jnp.where(lane < 64, m[0:1], m[1:2]),
                        jnp.where(lane < 64, m[2:3], m[3:4]),
                    ],
                    axis=1,
                )

            row = iota((32, 256), 0)
            mask = jnp.where(row < 4, along(three[0]), jnp.where(row < 20, along(three[1]), along(three[2])))
            masked = recv_ref[z].astype(F32) * mask
            column = iota((32, 256), 1)
            before = jnp.where(column == 0, 0.0, pltpu.roll(masked, 1, 1))
            after = jnp.where(column == 255, 0.0, pltpu.roll(masked, 255, 1))
            shifted += [before, masked, after, jnp.zeros((32, 256), F32)]
        shifted = jnp.concatenate(shifted, axis=0).astype(BF16)
        turned = lax.dot_general(perm4[...], shifted, NT, preferred_element_type=F32).astype(BF16)
        for u in range(2):
            embedded = dot(turned[:, 128 * u : 128 * u + 128], w_e[...])
            planes[u] = jnp.maximum(embedded, 0.0).astype(BF16)

        def windows(low, high):
            return jnp.concatenate(
                [
                    jnp.concatenate(
                        [planes[u, 128 * (p + b) : 128 * (p + b) + 128, low:high] for b in range(3)],
                        axis=1,
                    )
                    for u in range(2)
                    for p in range(2)
                ],
                axis=0,
            )

        def keep(summed, first, width, marks_of):
            for u in range(2):
                z = 2 * step + u
                rows_of = marks_of(marks[u])
                for p in range(2):
                    for y in range(4):
                        at = 128 * p + 32 * y
                        piece = summed[256 * u + at : 256 * u + at + 32]
                        piece = jnp.maximum(piece, 0.0) * rows_of[y]
                        feats[z, at : at + 32, first : first + width] = piece.astype(BF16)

        def inner(three):
            return [jnp.concatenate([three[1][y : y + 1]] * 2, axis=1) for y in range(4)]

        def outer(three):
            return [jnp.where(lane < 64, three[0][y : y + 1], three[2][y : y + 1]) for y in range(4)]

        keep(dot(windows(0, 384), w_c[...]), 0, 256, inner)
        keep(dot(windows(256, 640), w_c[...]), 256, 256, inner)
        keep(dot(windows(512, 768), w_h[...]), 512, 128, outer)

        def pairs(spans):
            return jnp.concatenate(
                [
                    jnp.concatenate(
                        [
                            feats[2 * step + u, 128 * p : 128 * p + 128, low:high]
                            for p in range(2)
                            for low, high in spans
                        ],
                        axis=1,
                    )
                    for u in range(2)
                ],
                axis=0,
            )

        lowered = [
            dot(pairs([(0, 256), (512, 640)]), w_d0[...]),
            dot(pairs([(128, 512)]), w_d1[...]),
            dot(pairs([(384, 640)]), w_d2[...]),
        ]
        for u in range(2):
            left, middle, right = marks[u]
            for y in range(4):
                m = middle[y : y + 1]
                rows_of = [
                    jnp.concatenate([jnp.where(lane < 64, left[y : y + 1], m), m], axis=1),
                    jnp.concatenate([m, m], axis=1),
                    jnp.where(lane < 64, m, right[y : y + 1]),
                ]
                for part, width in ((0, 256), (1, 256), (2, 128)):
                    piece = lowered[part][128 * u + 32 * y : 128 * u + 32 * y + 32]
                    piece = jnp.maximum(piece, 0.0) * rows_of[part]
                    tall[u, 8 + 32 * y : 40 + 32 * y, 256 * part : 256 * part + width] = piece
            for b in range(3):
                downs[2 * step + u, b] = tall[u, 7 + b : 135 + b, :].astype(BF16)

    @pl.loop(0, nz // 2)
    def _(step):
        middle = masks_ref[4]
        rows_of = [jnp.concatenate([middle[y : y + 1]] * 2, axis=1) for y in range(4)]
        gathered = jnp.concatenate(
            [
                jnp.concatenate(
                    [
                        downs[2 * step + u + s, b, :, 256 * g : 256 * g + 384]
                        for s in range(3)
                        for b in range(3)
                    ],
                    axis=1,
                )
                for g in range(2)
                for u in range(2)
            ],
            axis=0,
        )
        deep_sum = dot(gathered, w_z[...])
        deep = jnp.concatenate(
            [
                jnp.maximum(deep_sum[32 * r : 32 * r + 32], 0.0) * rows_of[r % 4]
                for r in range(16)
            ],
            axis=0,
        ).astype(BF16)
        raised = dot(deep, w_u[...])
        for g in range(2):
            for u in range(2):
                for p in range(2):
                    for y in range(4):
                        at = 128 * p + 32 * y
                        row = 256 * g + 128 * u + 32 * y
                        piece = raised[row : row + 32, 256 * p : 256 * p + 256]
                        skip = feats[2 * step + u + 1, at : at + 32, 256 * g : 256 * g + 256]
                        piece = jnp.maximum(piece + skip.astype(F32), 0.0) * rows_of[y]
                        decoded[u, at : at + 32, 256 * g : 256 * g + 256] = piece.astype(BF16)
        halves = []
        for u in range(2):
            projected = lax.dot_general(w_o[...], decoded[u], NT, preferred_element_type=F32)
            high = projected.astype(BF16)
            halves += [high, (projected - high.astype(F32)).astype(BF16)]
        ordered = dot(jnp.concatenate(halves, axis=0), perm_out[...])
        y_mask = jnp.concatenate(
            [
                jnp.where(lane < 64, middle[0:1], middle[1:2]),
                jnp.where(lane < 64, middle[2:3], middle[3:4]),
            ],
            axis=1,
        )
        for u in range(2):
            both = (ordered[96 * u : 96 * u + 48] + ordered[96 * u + 48 : 96 * u + 96]) * y_mask
            for d in range(3):
                logits_ref[d, 2 * step + u] = both[16 * d : 16 * d + 16]


def network(recv, masks, w_emb, w_one, w_down, w_deep, w_up, w_out, blk, nb, interpret=False):
    nz, length_y = nb, recv.shape[2]
    emb = jnp.tile(jnp.transpose(w_emb, (1, 2, 0)).reshape(9, 32), (1, 4))
    one = jnp.transpose(w_one, (2, 3, 0, 1))
    down = jnp.tile(jnp.transpose(w_down, (3, 2, 1, 0)).reshape(4, 32, 64), (1, 1, 2))
    deep = jnp.transpose(w_deep, (2, 3, 4, 0, 1))
    up = jnp.transpose(w_up, (3, 2, 0, 1)).reshape(2, 64, 64)
    out_w = jnp.tile(w_out, (1, 4))
    return pl.pallas_call(
        functools.partial(network_kernel, nb),
        out_shape=jax.ShapeDtypeStruct((3, nz, 16, length_y), F32),
        in_specs=[pl.BlockSpec(memory_space=pltpu.VMEM)] * 8
        + [pl.BlockSpec(memory_space=pltpu.SMEM)],
        out_specs=pl.BlockSpec(memory_space=pltpu.VMEM),
        scratch_shapes=[
            pltpu.VMEM((512, 256), BF16),
            pltpu.VMEM((256, 256), BF16),
            pltpu.VMEM((128, 768), BF16),
            pltpu.VMEM((1152, 256), BF16),
            pltpu.VMEM((768, 128), BF16),
            pltpu.VMEM((768, 256), BF16),
            pltpu.VMEM((768, 256), BF16),
            pltpu.VMEM((512, 128), BF16),
            pltpu.VMEM((3456, 256), BF16),
            pltpu.VMEM((256, 512), BF16),
            pltpu.VMEM((48, 512), BF16),
            pltpu.VMEM((27, 64, 128), F32),
            pltpu.VMEM((9, 32, 128), F32),
            pltpu.VMEM((2, 512, 768), BF16),
            pltpu.VMEM((nz + 2, 256, 640), BF16),
            pltpu.VMEM((2, 144, 640), F32),
            pltpu.VMEM((nz + 2, 3, 128, 640), BF16),
            pltpu.VMEM((2, 256, 512), BF16),
        ],
        compiler_params=pltpu.CompilerParams(vmem_limit_bytes=56 * 1024 * 1024),
        name="network",
        interpret=interpret,
    )(recv, masks, emb, one, down, deep, up, out_w, blk)


def solution(mesh):
    ns, nb = mesh.shape["sec"], mesh.shape["blk"]

    def per_device(raw, tissue, *weights):
        recv, masks = exchange(raw, tissue, ns, nb)
        blk = jnp.full((1,), lax.axis_index("blk"), jnp.int32)
        return network(recv, masks, *weights, blk, nb)

    placed = (P(("sec", "blk"), None, None), P("sec", "blk", None), P(), P(), P(), P(), P(), P())
    return jax.shard_map(
        per_device,
        mesh=mesh,
        in_specs=placed,
        out_specs=P(None, "sec", "blk", None),
        check_vma=False,
    )
```

time: 190 us -> 39.1 us (0.21)
  the two profiles are of different devices: /device:TPU:11 before, /device:TPU:0 now
where the time goes in v1:
time: 39.1 us; the launch traced here: 38.8 us
  Pallas kernels  34.6 us (88%)
  local copies, waits for them, and re-layouts  4.16 us (11%)
    pallas_call x1, Pallas kernels, network(): pl.pallas_call(functools.partial(network_kernel, nb), out_shape=jax.Shape...  23.1 us
    pallas_call x1, Pallas kernels, exchange(): pl.pallas_call(functools.partial(exchange_kernel, ns, nb), out_shape=(jax...  11.5 us
    another operation x3, local copies, waits for them, and re-layouts, network(): emb = jnp.tile(jnp.transpose(w_emb, (1, 2, 0)).reshape(9, 32), (1, 4))  1.39 us
    another operation x2, local copies, waits for them, and re-layouts, network(): out_w = jnp.tile(w_out, (1, 4))  1.37 us

profile of v1, /device:TPU:0, one launch (start us, length us, event | category | flops | bytes accessed | tf_op | source)
XLA Modules:
  0.0 38.8 jit_solution(10518820951672817013)
XLA Ops:
  0.0 0.0 copy-start
  0.0 0.7 %tile.35 = bf16[3,4,32]{2,1,0:T(4,128)(2,1)S(1)} broadcast(bf16[3,32]{1,0:T(4,128)(2,1)} %param.15), dimensions={0,2} | broadcast | bytes 960 | tf_op jit(solution)/shard_map/tile | solution.py:492
  0.7 0.7 %tile.36.out_w_ref = bf16[3,128]{1,0:T(4,128)(2,1)} reshape(bf16[3,4,32]{2,1,0:T(4,128)(2,1)S(1)} %tile.35) | data formatting | bytes 1536 | tf_op jit(solution)/shard_map/tile | solution.py:492
  1.4 0.7 %tile.29 = bf16[9,32]{1,0:T(8,128)(2,1)S(1)} reshape(bf16[3,3,32]{2,1,0:T(4,128)(2,1)} %bitcast.14) | data formatting | bytes 1152 | tf_op jit(solution)/shard_map/tile | solution.py:487
  2.1 0.7 %tile.31.emb_ref = bf16[9,128]{1,0:T(8,128)(2,1)} reshape(bf16[9,4,32]{2,1,0:T(4,128)(2,1)S(1)} %tile.30) | data formatting | bytes 4608 | tf_op jit(solution)/shard_map/tile | solution.py:487
  2.8 0.0 copy-done
  2.8 0.0 copy-start.1
  2.8 0.7 %tile.34.down_ref = bf16[4,32,128]{2,1,0:T(8,128)(2,1)} reshape(bf16[4,32,2,64]{3,2,1,0:T(2,128)(2,1)S(1)} %tile.33) | data formatting | bytes 65536 | tf_op jit(solution)/shard_map/tile | solution.py:489
  3.5 0.1 copy-done.1
  3.6 0.6 %copy.11 = bf16[2,2,32,64]{3,2,1,0:T(8,128)(2,1)} copy(bf16[2,2,32,64]{3,0,1,2:T(2,128)(2,1)S(1)} %bitcast.13) | data formatting | bytes 32768 | tf_op jit(solution)/shard_map/transpose | solution.py:491
  4.2 11.5 %exchange.1 = (bf16[10,32,256]{2,1,0:T(8,128)(2,1)}, f32[9,8,128]{2,1,0:T(8,128)}) custom-call(bf16[1,128,256]{2,1,0:T(8,128)(2,1)} %raw_ref.1, s32[1,1,4]{2,1,0:T(1,128)} %tissue_ref.1), custom_call_target="tpu_custom_call" | custom-call | tf_op jit(solution)/shard_map/exchange/pallas_call | solution.py:172
  15.7 23.1 %network.1 = f32[3,8,16,256]{3,2,1,0:T(8,128)} custom-call(bf16[10,32,256]{2,1,0:T(8,128)(2,1)} %get-tuple-element.7.recv_ref, f32[9,8,128]{2,1,0:T(8,128)} %get-tuple-element.8.masks_ref, bf16[9,128]{1,0:T(8,128)(2,1)} %tile.31.emb_ref, bf16[3,3,32,32]{3,2,1,0:T(8,128)(2,1)} %bitcast.12, bf16[4,32,128]{2,1,0:T(8,128)(2,1)} %tile.34.down_ref, ...), custom_call_target="tpu_custom_call" | custom-call | tf_op jit(solution)/shard_map/network/pallas_call | solution.py:493
  (3 shorter events, 0.1 us)
Async XLA Ops:
  0.0 2.8 %copy-start = (bf16[64,32,2,2]{0,3,2,1:T(2,128)(2,1)S(1)}, bf16[64,32,2,2]{0,3,2,1:T(2,128)(2,1)}, u32[]{:S(2)}) copy-start(bf16[64,32,2,2]{0,3,2,1:T(2,128)(2,1)} %param.12) | copy-start | bytes 49156
  2.8 0.8 %copy-start.1 = (bf16[32,64,2,2]{1,3,2,0:T(2,128)(2,1)S(1)}, bf16[32,64,2,2]{1,3,2,0:T(2,128)(2,1)}, u32[]{:S(2)}) copy-start(bf16[32,64,2,2]{1,3,2,0:T(2,128)(2,1)} %param.14) | copy-start | bytes 49156

commit v2 on v1

--- a/solution.py
+++ b/solution.py
@@ -205,7 +205,7 @@
 
 def network_kernel(
     nb, recv_ref, masks_ref, emb_ref, one_ref, down_ref, deep_ref, up_ref, out_w_ref, blk_ref,
-    logits_ref, perm4, perm_out, w_e, w_c, w_h, w_d0, w_d1, w_d2, w_z, w_u, w_o, deep_t, one_t,
+    logits_ref, perm_out, w_e, w_c, w_h, w_d0, w_d1, w_d2, w_z, w_u, w_o, deep_t, one_t, down_t,
     planes, feats, tall, downs, decoded
 ):
     nz = nb
@@ -224,14 +224,17 @@
             total = jnp.zeros((rows, 128), F32)
         dst[row : row + rows, 128 * tile : 128 * tile + 128] = total.astype(BF16)
 
-    y_of = iota((512, 256), 0)
-    perm4[...] = jnp.where(
-        iota((512, 256), 1) == 2 * (y_of % 128) - 1 + y_of // 128, 1.0, 0.0
-    ).astype(BF16)
     row_of = iota((256, 256), 0)
     perm_out[...] = jnp.where(
         iota((256, 256), 1) == 2 * (row_of % 128) + row_of // 128, 1.0, 0.0
     ).astype(BF16)
+
+    dup32 = jnp.where(iota((32, 128), 0) == iota((32, 128), 1) % 32, 1.0, 0.0).astype(BF16)
+    dup64 = jnp.where(iota((64, 128), 0) == iota((64, 128), 1) % 64, 1.0, 0.0).astype(BF16)
+    for at in range(4):
+        down_t[at] = dot(down_ref[at], dup64)
+    emb_rows = [dot(emb_ref[a], dup32) for a in range(3)]
+    out_rows = dot(out_w_ref[...], dup32)
 
     first_x = 16 * blk_ref[0]
     for tile in range(6):
@@ -240,7 +243,7 @@
         for b in range(3):
             total = jnp.zeros((32, 128), F32)
             for a in range(3):
-                weight = emb_ref[a * 3 + b : a * 3 + b + 1, :].astype(F32)
+                weight = emb_rows[a][b : b + 1, :]
                 hit = jnp.logical_and(iota((32, 128), 0) == x_of + a + 3, inside)
                 total = jnp.where(hit, weight, total)
             w_e[32 * b : 32 * b + 32, 128 * tile : 128 * tile + 128] = total.astype(BF16)
@@ -263,21 +266,20 @@
             )
 
     def one_block(b, a):
-        return (lambda: one_t[b * 3 + a]) if 0 <= a <= 2 else None
-
-    for b in range(3):
-        for e in range(12):
-            for tile in range(2):
-                blocks = [one_block(b, e - 4 * tile - q) for q in range(4)]
-                put(w_c, (b * 12 + e) * 32, 32, tile, 32, blocks)
-        for e in range(4):
-            pair = [one_block(b, e), one_block(b, e - 1)]
-            put(w_h, (b * 8 + e) * 32, 32, 0, 32, [None, None] + pair)
-            put(w_h, (b * 8 + 4 + e) * 32, 32, 0, 32, pair + [None, None])
+        return (lambda: one_t[b * 3 + a]) if 0 <= a <= 2 and 0 <= b <= 2 else None
+
+    for k in range(4):
+        for p in range(2):
+            for e in range(8):
+                put(w_c, (k * 8 + e) * 32, 32, p, 32, [one_block(k - p, e - q) for q in range(4)])
+            for e in range(4):
+                pair = [one_block(k - p, e), one_block(k - p, e - 1)]
+                put(w_h, (k * 8 + e) * 32, 32, p, 32, [None, None] + pair)
+                put(w_h, (k * 8 + 4 + e) * 32, 32, p, 32, pair + [None, None])
 
     def down_block(p, x, half):
         a = x - 2 * half
-        return (lambda: down_ref[p * 2 + a].astype(F32)) if 0 <= a <= 1 else None
+        return (lambda: down_t[p * 2 + a]) if 0 <= a <= 1 else None
 
     rims = [-2, -1, 16, 17]
     for dst, columns, halves in (
@@ -292,14 +294,14 @@
                     put(dst, (p * len(columns) + at) * 32, 32, tile, 64, blocks)
 
     def deep_block(s, b, a):
-        return (lambda: deep_t[(s * 3 + b) * 3 + a]) if 0 <= a <= 2 else None
-
-    for s in range(3):
+        return (lambda: deep_t[(s * 3 + b) * 3 + a]) if 0 <= a <= 2 and 0 <= s <= 2 else None
+
+    for k in range(4):
         for b in range(3):
-            for e in range(6):
+            for e in range(4):
                 for tile in range(2):
-                    blocks = [deep_block(s, b, e - 2 * tile - q) for q in range(2)]
-                    put(w_z, ((s * 3 + b) * 6 + e) * 64, 64, tile, 64, blocks)
+                    blocks = [deep_block(k - tile, b, e - q) for q in range(2)]
+                    put(w_z, ((k * 3 + b) * 4 + e) * 64, 64, tile, 64, blocks)
 
     for p in range(2):
         block = up_ref[p]
@@ -313,24 +315,31 @@
 
     for tile in range(4):
         for d in range(3):
-            weight = out_w_ref[d : d + 1, :].astype(F32)
+            weight = out_rows[d : d + 1, :]
             w_o[16 * d : 16 * d + 16, 128 * tile : 128 * tile + 128] = jnp.where(
                 iota((16, 128), 0) == lane // 32 + 4 * tile, weight, 0.0
             ).astype(BF16)
 
     for u in range(2):
-        tall[u, 0:8, :] = jnp.zeros((8, 640), F32)
-        tall[u, 136:144, :] = jnp.zeros((8, 640), F32)
-
-    @pl.loop(0, (nz + 2) // 2)
-    def _(step):
+        for slot in range(2):
+            tall[slot, u, 0:8, :] = jnp.zeros((8, 640), F32)
+            tall[slot, u, 136:144, :] = jnp.zeros((8, 640), F32)
+
+    def marks_at(step):
         marks = []
+        for u in range(2):
+            z = 2 * step + u
+            zone = 0 if z == 0 else (2 if z == nz + 1 else 1)
+            marks.append([masks_ref[zone * 3 + k] for k in range(3)])
+        return marks
+
+    def embed(step):
+        marks = marks_at(step)
+        slot = step % 2
         shifted = []
         for u in range(2):
             z = 2 * step + u
-            zone = jnp.where(z == 0, 0, jnp.where(z == nz + 1, 2, 1))
-            three = [masks_ref[zone * 3 + k] for k in range(3)]
-            marks.append(three)
+            three = marks[u]
 
             def along(m):
                 return jnp.concatenate(
@@ -349,44 +358,58 @@
             after = jnp.where(column == 255, 0.0, pltpu.roll(masked, 255, 1))
             shifted += [before, masked, after, jnp.zeros((32, 256), F32)]
         shifted = jnp.concatenate(shifted, axis=0).astype(BF16)
-        turned = lax.dot_general(perm4[...], shifted, NT, preferred_element_type=F32).astype(BF16)
+        turned = lax.dot_general(perm_out[...], shifted, NT, preferred_element_type=F32).astype(BF16)
         for u in range(2):
-            embedded = dot(turned[:, 128 * u : 128 * u + 128], w_e[...])
-            planes[u] = jnp.maximum(embedded, 0.0).astype(BF16)
-
-        def windows(low, high):
+            embedded = jnp.maximum(dot(turned[:, 128 * u : 128 * u + 128], w_e[...]), 0.0)
+            even, odd = embedded[:128], embedded[128:]
+            j = iota((128, 768), 0)
+            planes[slot, u, 0:128] = jnp.where(j == 0, 0.0, pltpu.roll(odd, 1, 0)).astype(BF16)
+            planes[slot, u, 128:256] = even.astype(BF16)
+            planes[slot, u, 256:384] = odd.astype(BF16)
+            planes[slot, u, 384:512] = jnp.where(j == 127, 0.0, pltpu.roll(even, 127, 0)).astype(BF16)
+
+    def convolve(step):
+        marks = marks_at(step)
+        slot = step % 2
+
+        def windows(tiles):
             return jnp.concatenate(
                 [
                     jnp.concatenate(
-                        [planes[u, 128 * (p + b) : 128 * (p + b) + 128, low:high] for b in range(3)],
+                        [planes[slot, u, 128 * k : 128 * k + 128, 128 * t : 128 * t + 256] for k in range(4)],
                         axis=1,
                     )
                     for u in range(2)
-                    for p in range(2)
+                    for t in tiles
                 ],
                 axis=0,
             )
 
-        def keep(summed, first, width, marks_of):
+        def keep(summed, tiles, rows_of):
             for u in range(2):
                 z = 2 * step + u
-                rows_of = marks_of(marks[u])
-                for p in range(2):
-                    for y in range(4):
-                        at = 128 * p + 32 * y
-                        piece = summed[256 * u + at : 256 * u + at + 32]
-                        piece = jnp.maximum(piece, 0.0) * rows_of[y]
-                        feats[z, at : at + 32, first : first + width] = piece.astype(BF16)
-
-        def inner(three):
-            return [jnp.concatenate([three[1][y : y + 1]] * 2, axis=1) for y in range(4)]
-
-        def outer(three):
-            return [jnp.where(lane < 64, three[0][y : y + 1], three[2][y : y + 1]) for y in range(4)]
-
-        keep(dot(windows(0, 384), w_c[...]), 0, 256, inner)
-        keep(dot(windows(256, 640), w_c[...]), 256, 256, inner)
-        keep(dot(windows(512, 768), w_h[...]), 512, 128, outer)
+                for at, t in enumerate(tiles):
+                    for p in range(2):
+                        for y in range(4):
+                            row = (u * len(tiles) + at) * 128 + 32 * y
+                            piece = summed[row : row + 32, 128 * p : 128 * p + 128]
+                            piece = jnp.maximum(piece, 0.0) * rows_of(marks[u], y)
+                            feats[
+                                z, 128 * p + 32 * y : 128 * p + 32 * y + 32, 128 * t : 128 * t + 128
+                            ] = piece.astype(BF16)
+
+        def inner(three, y):
+            return three[1][y : y + 1]
+
+        def outer(three, y):
+            return jnp.where(lane < 64, three[0][y : y + 1], three[2][y : y + 1])
+
+        keep(dot(windows(range(4)), w_c[...]), range(4), inner)
+        keep(dot(windows([4]), w_h[...]), [4], outer)
+
+    def lower(step):
+        marks = marks_at(step)
+        slot = step % 2
 
         def pairs(spans):
             return jnp.concatenate(
@@ -421,26 +444,34 @@
                 for part, width in ((0, 256), (1, 256), (2, 128)):
                     piece = lowered[part][128 * u + 32 * y : 128 * u + 32 * y + 32]
                     piece = jnp.maximum(piece, 0.0) * rows_of[part]
-                    tall[u, 8 + 32 * y : 40 + 32 * y, 256 * part : 256 * part + width] = piece
+                    tall[slot, u, 8 + 32 * y : 40 + 32 * y, 256 * part : 256 * part + width] = piece
             for b in range(3):
-                downs[2 * step + u, b] = tall[u, 7 + b : 135 + b, :].astype(BF16)
-
-    @pl.loop(0, nz // 2)
-    def _(step):
+                downs[2 * step + u, b] = tall[slot, u, 7 + b : 135 + b, :].astype(BF16)
+
+    steps = (nz + 2) // 2
+    for at in range(steps + 2):
+        if at < steps:
+            embed(at)
+        if 0 <= at - 1 < steps:
+            convolve(at - 1)
+        if at >= 2:
+            lower(at - 2)
+
+    def deepen(step):
         middle = masks_ref[4]
         rows_of = [jnp.concatenate([middle[y : y + 1]] * 2, axis=1) for y in range(4)]
         gathered = jnp.concatenate(
             [
                 jnp.concatenate(
                     [
-                        downs[2 * step + u + s, b, :, 256 * g : 256 * g + 384]
-                        for s in range(3)
+                        downs[4 * step + 2 * v + k, b, :, 128 * t : 128 * t + 256]
+                        for k in range(4)
                         for b in range(3)
                     ],
                     axis=1,
                 )
-                for g in range(2)
-                for u in range(2)
+                for v in range(2)
+                for t in range(4)
             ],
             axis=0,
         )
@@ -448,24 +479,47 @@
         deep = jnp.concatenate(
             [
                 jnp.maximum(deep_sum[32 * r : 32 * r + 32], 0.0) * rows_of[r % 4]
-                for r in range(16)
+                for r in range(32)
             ],
             axis=0,
         ).astype(BF16)
+        deep = jnp.concatenate(
+            [
+                jnp.concatenate(
+                    [
+                        deep[
+                            (4 * v + 2 * g + h) * 128 : (4 * v + 2 * g + h) * 128 + 128,
+                            128 * w : 128 * w + 128,
+                        ]
+                        for h in range(2)
+                    ],
+                    axis=1,
+                )
+                for g in range(2)
+                for v in range(2)
+                for w in range(2)
+            ],
+            axis=0,
+        )
+        return deep
+
+    def decode(step, deep):
+        middle = masks_ref[4]
+        rows_of = [jnp.concatenate([middle[y : y + 1]] * 2, axis=1) for y in range(4)]
         raised = dot(deep, w_u[...])
         for g in range(2):
-            for u in range(2):
+            for u in range(4):
                 for p in range(2):
                     for y in range(4):
                         at = 128 * p + 32 * y
-                        row = 256 * g + 128 * u + 32 * y
+                        row = 512 * g + 128 * u + 32 * y
                         piece = raised[row : row + 32, 256 * p : 256 * p + 256]
-                        skip = feats[2 * step + u + 1, at : at + 32, 256 * g : 256 * g + 256]
+                        skip = feats[4 * step + u + 1, at : at + 32, 256 * g : 256 * g + 256]
                         piece = jnp.maximum(piece + skip.astype(F32), 0.0) * rows_of[y]
-                        decoded[u, at : at + 32, 256 * g : 256 * g + 256] = piece.astype(BF16)
+                        decoded[step, u, at : at + 32, 256 * g : 256 * g + 256] = piece.astype(BF16)
         halves = []
-        for u in range(2):
-            projected = lax.dot_general(w_o[...], decoded[u], NT, preferred_element_type=F32)
+        for u in range(4):
+            projected = lax.dot_general(w_o[...], decoded[step, u], NT, preferred_element_type=F32)
             high = projected.astype(BF16)
             halves += [high, (projected - high.astype(F32)).astype(BF16)]
         ordered = dot(jnp.concatenate(halves, axis=0), perm_out[...])
@@ -476,20 +530,27 @@
             ],
             axis=1,
         )
-        for u in range(2):
+        for u in range(4):
             both = (ordered[96 * u : 96 * u + 48] + ordered[96 * u + 48 : 96 * u + 96]) * y_mask
             for d in range(3):
-                logits_ref[d, 2 * step + u] = both[16 * d : 16 * d + 16]
+                logits_ref[d, 4 * step + u] = both[16 * d : 16 * d + 16]
+
+    last = None
+    for step in range(nz // 4):
+        deep = deepen(step)
+        if last is not None:
+            decode(step - 1, last)
+        last = deep
+    decode(nz // 4 - 1, last)
 
 
 def network(recv, masks, w_emb, w_one, w_down, w_deep, w_up, w_out, blk, nb, interpret=False):
     nz, length_y = nb, recv.shape[2]
-    emb = jnp.tile(jnp.transpose(w_emb, (1, 2, 0)).reshape(9, 32), (1, 4))
+    emb = jnp.transpose(w_emb, (1, 2, 0))
     one = jnp.transpose(w_one, (2, 3, 0, 1))
-    down = jnp.tile(jnp.transpose(w_down, (3, 2, 1, 0)).reshape(4, 32, 64), (1, 1, 2))
+    down = jnp.transpose(w_down, (3, 2, 1, 0)).reshape(4, 32, 64)
     deep = jnp.transpose(w_deep, (2, 3, 4, 0, 1))
     up = jnp.transpose(w_up, (3, 2, 0, 1)).reshape(2, 64, 64)
-    out_w = jnp.tile(w_out, (1, 4))
     return pl.pallas_call(
         functools.partial(network_kernel, nb),
         out_shape=jax.ShapeDtypeStruct((3, nz, 16, length_y), F32),
@@ -497,29 +558,29 @@
         + [pl.BlockSpec(memory_space=pltpu.SMEM)],
         out_specs=pl.BlockSpec(memory_space=pltpu.VMEM),
         scratch_shapes=[
-            pltpu.VMEM((512, 256), BF16),
             pltpu.VMEM((256, 256), BF16),
             pltpu.VMEM((128, 768), BF16),
-            pltpu.VMEM((1152, 256), BF16),
-            pltpu.VMEM((768, 128), BF16),
+            pltpu.VMEM((1024, 256), BF16),
+            pltpu.VMEM((1024, 256), BF16),
             pltpu.VMEM((768, 256), BF16),
             pltpu.VMEM((768, 256), BF16),
             pltpu.VMEM((512, 128), BF16),
-            pltpu.VMEM((3456, 256), BF16),
+            pltpu.VMEM((3072, 256), BF16),
             pltpu.VMEM((256, 512), BF16),
             pltpu.VMEM((48, 512), BF16),
             pltpu.VMEM((27, 64, 128), F32),
             pltpu.VMEM((9, 32, 128), F32),
-            pltpu.VMEM((2, 512, 768), BF16),
+            pltpu.VMEM((4, 32, 128), F32),
+            pltpu.VMEM((2, 2, 512, 768), BF16),
             pltpu.VMEM((nz + 2, 256, 640), BF16),
-            pltpu.VMEM((2, 144, 640), F32),
+            pltpu.VMEM((2, 2, 144, 640), F32),
             pltpu.VMEM((nz + 2, 3, 128, 640), BF16),
-            pltpu.VMEM((2, 256, 512), BF16),
+            pltpu.VMEM((nz // 4, 4, 256, 512), BF16),
         ],
         compiler_params=pltpu.CompilerParams(vmem_limit_bytes=56 * 1024 * 1024),
         name="network",
         interpret=interpret,
-    )(recv, masks, emb, one, down, deep, up, out_w, blk)
+    )(recv, masks, emb, one, down, deep, up, w_out, blk)
 
 
 def solution(mesh):

time: 39.1 us -> 27.8 us (0.71)
  Pallas kernels: 34.6 us -> 25.6 us
  local copies, waits for them, and re-layouts: 4.16 us -> 2 us
    pallas_call x1, Pallas kernels: 23.1 us -> 14.1 us  [network(): pl.pallas_call(functools.partial(network_kernel, nb), out_shape=jax.Shape...]
    another operation x7 -> x0, local copies, waits for them, and re-layouts: 3.49 us -> none  [the longest x3 1.39 us: network(): emb = jnp.tile(jnp.transpose(w_emb, (1, 2, 0)).reshape(9, 32), (1, 4))]
    transpose x0 -> x1, local copies, waits for them, and re-layouts: none -> 1.38 us  [network(): down = jnp.transpose(w_down, (3, 2, 1, 0)).reshape(4, 32, 64)]
where the time goes in v2:
time: 27.8 us; the launch traced here: 27.6 us
  Pallas kernels  25.6 us (92%)
  local copies, waits for them, and re-layouts  2 us (7%)
    pallas_call x1, Pallas kernels, network(): pl.pallas_call(functools.partial(network_kernel, nb), out_shape=jax.Shape...  14.1 us
    pallas_call x1, Pallas kernels, exchange(): pl.pallas_call(functools.partial(exchange_kernel, ns, nb), out_shape=(jax...  11.5 us
    transpose x1, local copies, waits for them, and re-layouts, network(): down = jnp.transpose(w_down, (3, 2, 1, 0)).reshape(4, 32, 64)  1.38 us
    transpose x1, local copies, waits for them, and re-layouts, network(): up = jnp.transpose(w_up, (3, 2, 0, 1)).reshape(2, 64, 64)  0.61 us

profile of v2, /device:TPU:0, one launch (start us, length us, event | category | flops | bytes accessed | tf_op | source)
XLA Modules:
  0.0 27.6 jit_solution(1314450361970529002)
XLA Ops:
  0.0 0.0 copy-start
  0.0 1.4 %copy.9 = bf16[2,2,32,64]{3,2,1,0:T(8,128)(2,1)} copy(bf16[2,2,32,64]{3,0,1,2:T(2,128)(2,1)} %bitcast.12) | data formatting | bytes 32768 | tf_op jit(solution)/shard_map/transpose | solution.py:551
  1.4 0.0 copy-done
  1.4 0.6 %copy.10 = bf16[2,2,32,64]{3,2,1,0:T(8,128)(2,1)} copy(bf16[2,2,32,64]{3,0,1,2:T(2,128)(2,1)S(1)} %bitcast.13) | data formatting | bytes 32768 | tf_op jit(solution)/shard_map/transpose | solution.py:553
  2.0 11.5 %exchange.1 = (bf16[10,32,256]{2,1,0:T(8,128)(2,1)}, f32[9,8,128]{2,1,0:T(8,128)}) custom-call(bf16[1,128,256]{2,1,0:T(8,128)(2,1)} %raw_ref.1, s32[1,1,4]{2,1,0:T(1,128)} %tissue_ref.1), custom_call_target="tpu_custom_call" | custom-call | tf_op jit(solution)/shard_map/exchange/pallas_call | solution.py:172
  13.5 14.1 %network.1 = f32[3,8,16,256]{3,2,1,0:T(8,128)} custom-call(bf16[10,32,256]{2,1,0:T(8,128)(2,1)} %get-tuple-element.7.recv_ref, f32[9,8,128]{2,1,0:T(8,128)} %get-tuple-element.8.masks_ref, bf16[3,3,32]{2,1,0:T(4,128)(2,1)} %bitcast.14, bf16[3,3,32,32]{3,2,1,0:T(8,128)(2,1)} %bitcast.11, bf16[4,32,64]{2,1,0:T(8,128)(2,1)} %bitcast.9, ...), custom_call_target="tpu_custom_call" | custom-call | tf_op jit(solution)/shard_map/network/pallas_call | solution.py:554
Async XLA Ops:
  0.0 1.4 %copy-start = (bf16[32,64,2,2]{1,3,2,0:T(2,128)(2,1)S(1)}, bf16[32,64,2,2]{1,3,2,0:T(2,128)(2,1)}, u32[]{:S(2)}) copy-start(bf16[32,64,2,2]{1,3,2,0:T(2,128)(2,1)} %param.14) | copy-start | bytes 49156
